TPU v7x, 32 devices: a whole 2x2x4 slice. The times are simulated.
32 devices in a mesh: row: 4 (over y, core), col: 8 (over z, x).
Axes of the slice: x: 2, y: 2, z: 4, core: 2. Of those that a mesh axis runs over, the one named last changes fastest.
Arguments:
- ainv_top: float32 [4096, 4096], P('row', 'col'), may hold values from -0.25 to 0.25
- par_struct: int32 [8, 16], replicated, may hold values from 0 to 31, as said below
- par_panel: float32 [8, 16, 128, 128], P('col', 'row'), may hold values from -6 to 6
- par_linv: float32 [8, 128, 128], P('col', 'row'), may hold values from -0.0625 to 0.0625
- par_dinv: float32 [8, 128, 128], P('col', 'row'), may hold values from -192 to 192
- kid_panel: float32 [16, 16, 128, 128], P('col', 'row'), may hold values from -6 to 6
- kid_upper: float32 [16, 128, 128], P('col', 'row'), may hold values from -6 to 6
- kid_linv: float32 [16, 128, 128], P('col', 'row'), may hold values from -0.0625 to 0.0625
- kid_dinv: float32 [16, 128, 128], P('col', 'row'), may hold values from -192 to 192
Outputs:
- par_offdiag: float32 [8, 16, 128, 128], P('col', 'row')
- par_diag: float32 [8, 128, 128], P('col', 'row')
- kid_offdiag: float32 [16, 16, 128, 128], P('col', 'row')
- kid_parent: float32 [16, 128, 128], P('col', 'row')
- kid_diag: float32 [16, 128, 128], P('col', 'row')
Inputs may be any that keep to these rules, and one draw needn't show every extreme that they name: `par_struct`: in every row, entries 2j and 2j + 1 are two different ancestors among j * 4 to (j + 1) * 4 - 1.
All inputs are finite; a program needn't handle non-finite values.
Results may differ from a plain program's by a relative error of at most 0.00014.
Values sent between devices are 32-bit elements; how exact they have to be, the bound alone decides.
No kernel may reach another device: no remote copies, remote signals or barrier semaphores. Data moves between devices by JAX's collectives and lax.ppermute only.
A program may use at most 128 MiB of HBM per device.

v0:
```python
import jax
import jax.numpy as jnp
from jax import lax
from jax.sharding import PartitionSpec as P

highest = lax.Precision.HIGHEST


def spread(array, axis, root):
    mine = lax.axis_index(axis) == root
    return lax.psum(jnp.where(mine, array, jnp.zeros_like(array)), axis)


def on_device(
    ainv_top, par_struct, par_panel, par_linv, par_dinv, kid_panel, kid_upper, kid_linv, kid_dinv
):
    grid_rows = lax.axis_size("row")
    grid_cols = lax.axis_size("col")
    my_row = lax.axis_index("row")
    my_col = lax.axis_index("col")
    tile_width = par_panel.shape[-1]
    band_rows = tile_width // grid_rows
    parents = par_panel.shape[0]
    slot_share = par_panel.shape[1]
    children = kid_panel.shape[0]
    brood = children // parents
    slots_all = par_struct.shape[1]
    pair_width = slots_all // grid_cols
    tile_rows = ainv_top.shape[0] // tile_width
    tile_cols = ainv_top.shape[1] // tile_width
    local_tiles = ainv_top.reshape(tile_rows, tile_width, tile_cols, tile_width)
    row_base = my_row * tile_rows
    col_base = my_col * tile_cols
    band_start = my_row * band_rows
    par_linv_full, par_dinv_full = (
        lax.all_gather(par_linv, "row", axis=1, tiled=True),
        lax.all_gather(par_dinv, "row", axis=1, tiled=True),
    )
    par_hat = jnp.einsum("psij,pjk->psik", par_panel, par_linv_full, precision=highest)
    owner_rows = lax.dynamic_slice_in_dim(par_struct, my_row * slot_share, slot_share, 1) - row_base
    owner_cols = lax.dynamic_slice_in_dim(par_struct, my_col * pair_width, pair_width, 1) - col_base
    root_row = my_col * pair_width // slot_share
    within = my_col * pair_width - root_row * slot_share
    every_hat = lax.all_gather(par_hat, "col", axis=0, tiled=True)
    picked = lax.dynamic_slice_in_dim(every_hat, within, pair_width, 1)
    picked = spread(picked, "row", root_row)
    rows_here = owner_rows
    cols_here = owner_cols
    picks_here = picked
    tiles_here = local_tiles[rows_here[:, :, None], :, cols_here[:, None, :], :]
    par_prod = lax.psum_scatter(
        jnp.einsum("pjkab,pkbc->pjac", tiles_here, picks_here, precision=highest),
        "col",
        scatter_dimension=0,
        tiled=True,
    )
    par_off = -par_prod
    pivot_term = jnp.einsum(
        "pji,pjk,pkl->pil", par_linv_full, par_dinv_full, par_linv_full, precision=highest
    )
    diag_part = -jnp.einsum("psji,psjk->pik", par_hat, par_off, precision=highest)
    par_diag_full = pivot_term + lax.psum(diag_part, "row")
    par_diag_band = lax.dynamic_slice_in_dim(par_diag_full, band_start, band_rows, 1)
    kid_upper_full, kid_linv_full, kid_dinv_full = (
        lax.all_gather(kid_upper, "row", axis=1, tiled=True),
        lax.all_gather(kid_linv, "row", axis=1, tiled=True),
        lax.all_gather(kid_dinv, "row", axis=1, tiled=True),
    )
    kid_hat = jnp.einsum("csij,cjk->csik", kid_panel, kid_linv_full, precision=highest)
    kid_uphat = jnp.einsum("cij,cjk->cik", kid_upper_full, kid_linv_full, precision=highest)
    kid_rows = jnp.repeat(owner_rows, brood, axis=0)
    kid_cols = jnp.repeat(owner_cols, brood, axis=0)
    every_kid = lax.all_gather(kid_hat, "col", axis=0, tiled=True)
    kid_picked = lax.dynamic_slice_in_dim(every_kid, within, pair_width, 1)
    kid_picked = spread(kid_picked, "row", root_row)
    rows_here = kid_rows
    cols_here = kid_cols
    picks_here = kid_picked
    tiles_here = local_tiles[rows_here[:, :, None], :, cols_here[:, None, :], :]
    kid_prod = lax.psum_scatter(
        jnp.einsum("pjkab,pkbc->pjac", tiles_here, picks_here, precision=highest),
        "col",
        scatter_dimension=0,
        tiled=True,
    )
    uphat_grouped = kid_uphat.reshape(parents, brood, tile_width, tile_width)
    kid_off = -(
        kid_prod.reshape(parents, brood, slot_share, tile_width, tile_width)
        + jnp.einsum("pjab,pibc->pijac", par_off, uphat_grouped, precision=highest)
    )
    kid_off = kid_off.reshape(children, slot_share, tile_width, tile_width)
    linv_band = lax.dynamic_slice_in_dim(kid_linv_full, band_start, band_rows, 2)
    kid_pivot_band = jnp.einsum(
        "cji,cjk,ckl->cil", linv_band, kid_dinv_full, kid_linv_full, precision=highest
    )
    parent_part = jnp.einsum(
        "pjba,pijbc->piac",
        par_off,
        kid_hat.reshape(parents, brood, slot_share, tile_width, tile_width),
        precision=highest,
    ).reshape(children, tile_width, tile_width)
    hat_part = -jnp.einsum("csji,csjk->cik", kid_hat, kid_off, precision=highest)
    diag_times = jnp.einsum(
        "pab,pibc->piac", par_diag_full, uphat_grouped, precision=highest
    ).reshape(children, tile_width, tile_width)
    uphat_band = lax.dynamic_slice_in_dim(kid_uphat, band_start, band_rows, 2)
    parent_sum = lax.psum(parent_part, "row")
    kid_par_full = -(parent_sum + diag_times)
    diag_sum = lax.psum_scatter(hat_part, "row", scatter_dimension=1, tiled=True)
    kid_diag_band = (
        kid_pivot_band
        + diag_sum
        - jnp.einsum("cji,cjk->cik", uphat_band, kid_par_full, precision=highest)
    )
    kid_par_band = lax.dynamic_slice_in_dim(kid_par_full, band_start, band_rows, 1)
    return (par_off, par_diag_band, kid_off, kid_par_band, kid_diag_band)


def solution(mesh):
    placed = (
        P("row", "col"),
        P(),
        P("col", "row", None, None),
        P("col", "row", None),
        P("col", "row", None),
        P("col", "row", None, None),
        P("col", "row", None),
        P("col", "row", None),
        P("col", "row", None),
    )
    return jax.shard_map(
        on_device,
        mesh=mesh,
        in_specs=placed,
        out_specs=(
            P("col", "row", None, None),
            P("col", "row", None),
            P("col", "row", None, None),
            P("col", "row", None),
            P("col", "row", None),
        ),
        check_vma=False,
    )
```

profile of v0, /device:TPU:0, one launch (start us, length us, event | category | flops | bytes accessed | tf_op | source)
XLA Modules:
  0.0 442.1 jit_solution(8733068069592860143)
XLA Ops:
  7.2 0.0 all-gather.6.cloned.1.call-start
  7.2 6.6 %all_gather.21 = f32[1,128,128]{2,1,0:T(8,128)S(1)} all-gather(f32[1,32,128]{2,1,0:T(8,128)} %param.12), channel_id=1, replica_groups=mesh['row'=4,'col'=8] {'row'}, dimensions={1}, use_global_device_ids=true | all-gather | bytes 81920 | tf_op jit(solution)/shard_map/all_gather | solution.py:36
  13.8 0.6 copy-done.5
  14.4 2.0 fusion.14
  16.5 0.0 all-gather.6.cloned.1.call-update
  16.5 0.0 all-reduce.4.cloned.1.call-start
  16.6 51.1 %all-gather.6.cloned.1.call-done = f32[32,128,128]{2,1,0:T(8,128)} async-done(((f32[4,128,128]{2,1,0:T(8,128)}), f32[32,128,128]{2,1,0:T(8,128)}) %all-gather.6.cloned.1.call-update) | async-done | bytes 2097168 | tf_op jit(solution)/shard_map/all_gather | solution.py:44
  67.7 2.3 dynamic-slice_select_fusion.1
  70.0 0.0 all-reduce.4.cloned.1.call-update
  70.0 0.0 all-gather.4.cloned.1.call-start
  70.1 5.6 %all_gather.24 = f32[2,128,128]{2,1,0:T(8,128)S(1)} all-gather(f32[2,32,128]{2,1,0:T(8,128)} %param.16), channel_id=1, replica_groups=mesh['row'=4,'col'=8] {'row'}, dimensions={1}, use_global_device_ids=true | all-gather | bytes 163840 | tf_op jit(solution)/shard_map/all_gather | solution.py:66
  75.7 1.4 fusion.17
  77.1 0.0 all-gather.4.cloned.1.call-update
  77.1 0.0 reduce-scatter.4.cloned.1.call-start
  77.2 1.7 reshape.154
  78.9 1.9 copy.51
  80.8 0.1 fusion.33
  80.9 0.1 fusion.31
  81.0 0.1 broadcast_or_fusion.1
  81.1 0.1 reshape.129
  81.2 2.9 gather_fusion
  84.0 20.7 %all-reduce.4.cloned.1.call-done = f32[8,2,128,128]{3,2,1,0:T(8,128)} async-done(((f32[8,2,128,128]{3,2,1,0:T(8,128)}), f32[8,2,128,128]{3,2,1,0:T(8,128)}) %all-reduce.4.cloned.1.call-update) | async-done | bytes 1048592 | tf_op jit(solution)/shard_map/psum | solution.py:11
  104.7 7.5 %convolution_bitcast_fusion.1 = f32[8,4,128,128]{3,2,1,0:T(8,128)} fusion(f32[8,4,2,128,128]{4,3,2,1,0:T(8,128)} %bitcast.127, f32[8,2,128,128]{3,2,1,0:T(8,128)} %all-reduce.4.cloned.1.call-done), kind=kOutput, calls=%fused_computation.5 | convolution fusion | flops 1610612736 | bytes 7340032 | tf_op jit(solution)/shard_map/pjkab,pkbc->pjac/dot_general | solution.py:52
  112.3 0.0 reduce-scatter.4.cloned.1.call-update
  112.3 0.0 all-reduce.6.cloned.1.call-start
  112.3 69.1 %all-gather.4.cloned.1.call-done = f32[16,4,128,128]{3,2,1,0:T(8,128)} async-done(((f32[2,4,128,128]{3,2,1,0:T(8,128)}), f32[16,4,128,128]{3,2,1,0:T(8,128)}) %all-gather.4.cloned.1.call-update) | async-done | bytes 4194320 | tf_op jit(solution)/shard_map/all_gather | solution.py:73
  181.5 3.2 dynamic-slice_select_fusion
  184.7 66.5 %reduce-scatter.4.cloned.1.call-done = f32[1,4,128,128]{3,2,1,0:T(8,128)} async-done(((f32[8,4,128,128]{3,2,1,0:T(8,128)}), f32[1,4,128,128]{3,2,1,0:T(8,128)}) %reduce-scatter.4.cloned.1.call-update) | async-done | bytes 262160 | tf_op jit(solution)/shard_map/reduce_scatter | solution.py:51
  251.2 1.0 neg.18
  252.2 2.3 fusion.8
  254.5 1.7 convolution_bitcast_fusion.4
  256.1 0.0 all-reduce.6.cloned.1.call-update
  256.1 0.2 reduce-scatter.6.cloned.1.call-start
  256.4 0.1 copy.53
  256.4 0.1 broadcast_in_dim.39
  256.5 0.1 broadcast_in_dim_reshape.7
  256.6 0.6 fusion.37
  257.2 0.8 copy.54
  258.0 0.7 broadcast_or_fusion
  258.7 0.9 reshape.135
  259.6 4.5 %gather_fusion.1 = f32[128,128,128]{2,1,0:T(8,128)} fusion(f32[8,128,4,128]{3,1,2,0:T(8,128)S(1)} %copy.51, s32[128]{0:T(128)S(1)} %reshape.135), kind=kCustom, calls=%fused_computation.1 | custom fusion | bytes 16778240 | tf_op jit(solution)/shard_map/gather | solution.py:79
  264.0 46.2 %all-reduce.6.cloned.1.call-done = (f32[1,128,128]{2,1,0:T(8,128)}, f32[16,2,128,128]{3,2,1,0:T(8,128)}, f32[2,128,128]{1,2,0:T(8,128)}) async-done(((f32[1,128,128]{2,1,0:T(8,128)}, f32[16,2,128,128]{3,2,1,0:T(8,128)}, f32[2,128,128]{1,2,0:T(8,128)}), (f32[1,128,128]{2,1,0:T(8,128)}, f32[16,2,128,128]{3,2,1,0:T(8,128)}, f32[2,128,128]{1,2,0:T(8,128)})) %all-reduce.6.cloned.1.call-update) | async-done | bytes 2293776 | tf_op jit(solution)/shard_map/psum | solution.py:62
  310.3 12.1 %convolution_bitcast_fusion = f32[16,4,128,128]{3,2,1,0:T(8,128)} fusion(f32[16,4,2,128,128]{4,3,2,1,0:T(8,128)} %bitcast.126, f32[16,2,128,128]{3,2,1,0:T(8,128)} %get-tuple-element.26), kind=kOutput, calls=%fused_computation.2 | convolution fusion | flops 3221225472 | bytes 14680064 | tf_op jit(solution)/shard_map/pjkab,pkbc->pjac/dot_general | solution.py:81
  322.4 0.0 reduce-scatter.6.cloned.1.call-update
  322.4 0.0 reduce-scatter.8.cloned.1.call-start
  322.4 0.6 copy-done.11
  323.0 5.2 %all_gather.23 = f32[1,128,128]{2,1,0:T(8,128)S(1)} all-gather(f32[1,32,128]{2,1,0:T(8,128)S(1)} %copy-done.11), channel_id=1, replica_groups=mesh['row'=4,'col'=8] {'row'}, dimensions={1}, use_global_device_ids=true | all-gather | bytes 81920 | tf_op jit(solution)/shard_map/all_gather | solution.py:37
  328.3 5.4 %all_gather.26 = f32[2,128,128]{2,1,0:T(8,128)S(1)} all-gather(f32[2,32,128]{2,1,0:T(8,128)S(1)} %copy-done.9), channel_id=1, replica_groups=mesh['row'=4,'col'=8] {'row'}, dimensions={1}, use_global_device_ids=true | all-gather | bytes 163840 | tf_op jit(solution)/shard_map/all_gather | solution.py:65
  333.7 5.4 %all_gather.27 = f32[2,128,128]{2,1,0:T(8,128)S(1)} all-gather(f32[2,32,128]{2,1,0:T(8,128)S(1)} %copy-done.10), channel_id=1, replica_groups=mesh['row'=4,'col'=8] {'row'}, dimensions={1}, use_global_device_ids=true | all-gather | bytes 163840 | tf_op jit(solution)/shard_map/all_gather | solution.py:67
  339.1 0.4 fusion.19
  339.5 0.3 fusion.22
  339.8 0.4 fusion.38
  340.2 0.3 fusion.9
  340.5 70.0 %reduce-scatter.6.cloned.1.call-done = f32[2,4,128,128]{3,2,1,0:T(8,128)} async-done(((f32[16,4,128,128]{3,2,1,0:T(8,128)}), f32[2,4,128,128]{3,2,1,0:T(8,128)}) %reduce-scatter.6.cloned.1.call-update) | async-done | bytes 524304 | tf_op jit(solution)/shard_map/reduce_scatter | solution.py:80
  410.5 1.6 fusion.3
  412.2 1.7 fusion.4
  413.8 0.0 reduce-scatter.8.cloned.1.call-update
  413.9 0.3 fusion.6
  414.2 0.1 constant_dynamic-slice_fusion
  414.3 0.7 copy.63
  415.0 0.6 constant_dynamic-slice_fusion.1
  415.6 17.8 %reduce-scatter.8.cloned.1.call-done = f32[2,32,128]{2,1,0:T(8,128)} async-done(((f32[2,128,128]{2,1,0:T(8,128)}), f32[2,32,128]{2,1,0:T(8,128)}) %reduce-scatter.8.cloned.1.call-update) | async-done | bytes 32784 | tf_op jit(solution)/shard_map/reduce_scatter | solution.py:109
  433.4 1.0 convolution_add_fusion
  434.3 0.9 convolution_subtract_fusion
  (26 shorter events, 0.1 us)
Async XLA Ops:
  7.2 68.5 %copy-start = (f32[2,4,128,128]{3,2,1,0:T(8,128)S(1)}, f32[2,4,128,128]{3,2,1,0:T(8,128)}, u32[]{:S(2)}) copy-start(f32[2,4,128,128]{3,2,1,0:T(8,128)} %param.14) | copy-start | bytes 1572868
  7.2 70.0 %copy-start.3 = (f32[1024,512]{1,0:T(8,128)S(1)}, f32[1024,512]{1,0:T(8,128)}, u32[]{:S(2)}) copy-start(f32[1024,512]{1,0:T(8,128)} %param.9) | copy-start | bytes 6291460
  7.2 60.5 %all-gather.6.cloned.1.call-start = ((), (), s32[]{:S(2)}) async-start(), calls=%async_computation.8 | async-start | bytes 2359296 | tf_op jit(solution)/shard_map/all_gather | solution.py:44
  13.8 0.6 copy-start.5
  16.5 88.2 %all-reduce.4.cloned.1.call-start = ((), (), s32[]{:S(2)}) async-start(), calls=%async_computation.3 | async-start | bytes 2097152 | tf_op jit(solution)/shard_map/psum | solution.py:11
  70.0 111.5 %all-gather.4.cloned.1.call-start = ((), (), s32[]{:S(2)}) async-start(), calls=%async_computation.5 | async-start | bytes 4718592 | tf_op jit(solution)/shard_map/all_gather | solution.py:73
  77.1 174.1 %reduce-scatter.4.cloned.1.call-start = ((), (), s32[]{:S(2)}) async-start(), calls=%async_computation.4 | async-start | bytes 2359296 | tf_op jit(solution)/shard_map/reduce_scatter | solution.py:51
  77.2 3.6 copy-start.12
  112.3 142.2 %copy-start.1 = (f32[2,4,128,128]{3,2,1,0:T(8,128)S(1)}, f32[2,4,128,128]{3,2,1,0:T(8,128)}, u32[]{:S(2)}) copy-start(f32[2,4,128,128]{3,2,1,0:T(8,128)} %fusion.17) | copy-start | bytes 1572868
  112.3 198.0 %all-reduce.6.cloned.1.call-start = ((), (), s32[]{:S(2)}) async-start(), calls=%async_computation.9 | async-start | bytes 4587520 | tf_op jit(solution)/shard_map/psum | solution.py:62
  252.2 158.4 %copy-start.2 = (f32[1,4,128,128]{3,2,1,0:T(8,128)}, f32[1,4,128,128]{3,2,1,0:T(8,128)S(1)}, u32[]{:S(2)}) copy-start(f32[1,4,128,128]{3,2,1,0:T(8,128)S(1)} %neg.18) | copy-start | bytes 786436
  256.1 154.4 %reduce-scatter.6.cloned.1.call-start = ((), (), s32[]{:S(2)}) async-start(), calls=%async_computation.6 | async-start | bytes 4718592 | tf_op jit(solution)/shard_map/reduce_scatter | solution.py:80
  322.3 0.7 copy-start.11
  322.3 5.9 %copy-start.9 = (f32[2,32,128]{2,1,0:T(8,128)S(1)}, f32[2,32,128]{2,1,0:T(8,128)}, u32[]{:S(2)}) copy-start(f32[2,32,128]{2,1,0:T(8,128)} %param.15) | copy-start | bytes 98308
  322.3 11.4 %copy-start.10 = (f32[2,32,128]{2,1,0:T(8,128)S(1)}, f32[2,32,128]{2,1,0:T(8,128)}, u32[]{:S(2)}) copy-start(f32[2,32,128]{2,1,0:T(8,128)} %param.17) | copy-start | bytes 98308
  322.3 17.2 %copy-start.6 = (f32[1,128,128]{2,1,0:T(8,128)S(1)}, f32[1,128,128]{2,1,0:T(8,128)}, u32[]{:S(2)}) copy-start(f32[1,128,128]{2,1,0:T(8,128)} %copy-done.5) | copy-start | bytes 196612
  322.4 17.9 %copy-start.8 = (f32[1,128,128]{2,1,0:T(8,128)S(1)}, f32[1,128,128]{2,1,0:T(8,128)}, u32[]{:S(2)}) copy-start(f32[1,128,128]{2,1,0:T(8,128)} %get-tuple-element.25) | copy-start | bytes 196612
  322.4 91.5 %copy-start.7 = (f32[2,128,128]{1,2,0:T(8,128)S(1)}, f32[2,128,128]{1,2,0:T(8,128)}, u32[]{:S(2)}) copy-start(f32[2,128,128]{1,2,0:T(8,128)} %get-tuple-element.27) | copy-start | bytes 393220
  322.4 111.0 %reduce-scatter.8.cloned.1.call-start = ((), (), s32[]{:S(2)}) async-start(), calls=%async_computation.7 | async-start | bytes 163840 | tf_op jit(solution)/shard_map/reduce_scatter | solution.py:109
  412.2 23.1 %copy-start.4 = (f32[2,4,128,128]{3,2,1,0:T(8,128)}, f32[2,4,128,128]{3,2,1,0:T(8,128)S(1)}, u32[]{:S(2)}) copy-start(f32[2,4,128,128]{3,2,1,0:T(8,128)S(1)} %fusion.3) | copy-start | bytes 1572868
Sparse Core Ops, SparseCore 0:
  16.6 50.9 all-gather.5
  70.1 34.5 all-reduce.3
  107.7 73.7 all-gather.3
  185.3 65.8 reduce-scatter.3
  256.3 53.9 all-reduce.5
  322.5 87.9 reduce-scatter.5
  414.0 19.3 reduce-scatter.7
where the time goes:
time: 443 us; the launch traced here: 442 us
  waiting for transfers between devices  342 us (77%)
  matrix products  33.7 us (8%)
  blocking collectives  28.3 us (6%)
  local copies, waits for them, and re-layouts  15.7 us (4%)
  between operations  14.4 us (3%)
  other arithmetic  8.02 us (2%)
    reduce_scatter x2, waiting for transfers between devices, on_device(): lax.psum_scatter(jnp.einsum('pjkab,pkbc->pjac', tiles_here, picks_here, p...  137 us
    all_gather x1, waiting for transfers between devices, on_device(): every_kid = lax.all_gather(kid_hat, 'col', axis=0, tiled=True)  69.1 us
    all_gather x1, waiting for transfers between devices, on_device(): every_hat = lax.all_gather(par_hat, 'col', axis=0, tiled=True)  51.1 us
    psum x1, waiting for transfers between devices, on_device(): par_diag_full = pivot_term + lax.psum(diag_part, 'row')  46.2 us
    psum x1, waiting for transfers between devices, spread(): return lax.psum(jnp.where(mine, array, jnp.zeros_like(array)), axis)  20.7 us
    dot_general x2, matrix products, on_device(): jnp.einsum('pjkab,pkbc->pjac', tiles_here, picks_here, precision=highest)  19.6 us
    reduce_scatter x1, waiting for transfers between devices, on_device(): lax.psum_scatter(hat_part, 'row', scatter_dimension=1, tiled=True)  17.8 us
  transfers between devices with their start and end apart: 7, of which 7 were waited for; matrix products, arithmetic and copies ran while one was open for 7% of the time, Pallas kernels for 0%

commit v1 on v0

--- a/solution.py
+++ b/solution.py
@@ -41,7 +41,12 @@
     owner_cols = lax.dynamic_slice_in_dim(par_struct, my_col * pair_width, pair_width, 1) - col_base
     root_row = my_col * pair_width // slot_share
     within = my_col * pair_width - root_row * slot_share
-    every_hat = lax.all_gather(par_hat, "col", axis=0, tiled=True)
+    ring = [par_hat]
+    for hop in range(7):
+        ring.append(lax.ppermute(ring[-1], "col", [(dev, (dev + 1) % 8) for dev in range(8)]))
+    every_hat = jnp.roll(
+        jnp.concatenate(ring[::-1], axis=0), (lax.axis_index("col") + 1) * ring[0].shape[0], axis=0
+    )
     picked = lax.dynamic_slice_in_dim(every_hat, within, pair_width, 1)
     picked = spread(picked, "row", root_row)
     rows_here = owner_rows

time: 443 us -> 466 us (1.052)
  waiting for transfers between devices: 342 us -> 361 us
    ppermute x0 -> x7, waiting for transfers between devices: none -> 66.8 us  [on_device(): lax.ppermute(ring[-1], 'col', [(dev, (dev + 1) % 8) for dev in range(8)])]
    all_gather x1 -> x0, waiting for transfers between devices: 51.1 us -> none  [on_device(): every_hat = lax.all_gather(par_hat, 'col', axis=0, tiled=True)]
    unnamed x27 -> x52, local copies, waits for them, and re-layouts: 1.97 us -> 8.03 us
    psum x1, waiting for transfers between devices: 20.7 us -> 26.4 us  [spread(): return lax.psum(jnp.where(mine, array, jnp.zeros_like(array)), axis)]
    reduce_scatter x2, waiting for transfers between devices: 137 us -> 131 us  [on_device(): lax.psum_scatter(jnp.einsum('pjkab,pkbc->pjac', tiles_here, picks_here, p...]
  transfers between devices with their start and end apart: 7 -> 13, of which waited for: 7 -> 13; matrix products, arithmetic and copies ran while one was open for 7% -> 5% of each run, Pallas kernels for 0% -> 0%
where the time goes in v1:
time: 466 us; the launch traced here: 465 us
  waiting for transfers between devices  361 us (77%)
  matrix products  33.1 us (7%)
  blocking collectives  28.1 us (6%)
  local copies, waits for them, and re-layouts  20.3 us (4%)
  between operations  14.5 us (3%)
  other arithmetic  5.61 us (1%)
    reduce_scatter x2, waiting for transfers between devices, on_device(): lax.psum_scatter(jnp.einsum('pjkab,pkbc->pjac', tiles_here, picks_here, p...  131 us
    all_gather x1, waiting for transfers between devices, on_device(): every_kid = lax.all_gather(kid_hat, 'col', axis=0, tiled=True)  70.5 us
    ppermute x7, waiting for transfers between devices, on_device(): lax.ppermute(ring[-1], 'col', [(dev, (dev + 1) % 8) for dev in range(8)])  66.8 us
    psum x1, waiting for transfers between devices, on_device(): par_diag_full = pivot_term + lax.psum(diag_part, 'row')  48.1 us
    psum x1, waiting for transfers between devices, spread(): return lax.psum(jnp.where(mine, array, jnp.zeros_like(array)), axis)  26.4 us
    dot_general x2, matrix products, on_device(): jnp.einsum('pjkab,pkbc->pjac', tiles_here, picks_here, precision=highest)  19.7 us
    reduce_scatter x1, waiting for transfers between devices, on_device(): lax.psum_scatter(hat_part, 'row', scatter_dimension=1, tiled=True)  17.8 us
  transfers between devices with their start and end apart: 13, of which 13 were waited for; matrix products, arithmetic and copies ran while one was open for 5% of the time, Pallas kernels for 0%

profile of v1, /device:TPU:0, one launch (start us, length us, event | category | flops | bytes accessed | tf_op | source)
XLA Modules:
  0.0 465.0 jit_solution(12388048182553255253)
XLA Ops:
  7.2 6.6 %all_gather.18 = f32[1,128,128]{2,1,0:T(8,128)S(1)} all-gather(f32[1,32,128]{2,1,0:T(8,128)} %param.12), channel_id=1, replica_groups=mesh['row'=4,'col'=8] {'row'}, dimensions={1}, use_global_device_ids=true | all-gather | bytes 81920 | tf_op jit(solution)/shard_map/all_gather | solution.py:36
  13.8 1.3 fusion.14
  15.1 2.0 collective-permute-start
  17.1 9.8 %collective-permute-done = f32[1,4,128,128]{3,2,1,0:T(8,128)S(1)} collective-permute-done((f32[1,4,128,128]{3,2,1,0:T(8,128)S(1)}, f32[1,4,128,128]{3,2,1,0:T(8,128)S(1)}, u32[]{:S(2)}, u32[]{:S(2)}) %collective-permute-start) | collective-permute-done | bytes 262176 | tf_op jit(solution)/shard_map/ppermute | solution.py:46
  27.0 10.8 %collective-permute-done.1 = f32[1,4,128,128]{3,2,1,0:T(8,128)S(1)} collective-permute-done((f32[1,4,128,128]{3,2,1,0:T(8,128)S(1)}, f32[1,4,128,128]{3,2,1,0:T(8,128)S(1)}, u32[]{:S(2)}, u32[]{:S(2)}) %collective-permute-start.1) | collective-permute-done | bytes 262176 | tf_op jit(solution)/shard_map/ppermute | solution.py:46
  37.7 9.9 %collective-permute-done.2 = f32[1,4,128,128]{3,2,1,0:T(8,128)S(1)} collective-permute-done((f32[1,4,128,128]{3,2,1,0:T(8,128)S(1)}, f32[1,4,128,128]{3,2,1,0:T(8,128)S(1)}, u32[]{:S(2)}, u32[]{:S(2)}) %collective-permute-start.2) | collective-permute-done | bytes 262176 | tf_op jit(solution)/shard_map/ppermute | solution.py:46
  47.6 9.1 %collective-permute-done.3 = f32[1,4,128,128]{3,2,1,0:T(8,128)S(1)} collective-permute-done((f32[1,4,128,128]{3,2,1,0:T(8,128)S(1)}, f32[1,4,128,128]{3,2,1,0:T(8,128)S(1)}, u32[]{:S(2)}, u32[]{:S(2)}) %collective-permute-start.3) | collective-permute-done | bytes 262176 | tf_op jit(solution)/shard_map/ppermute | solution.py:46
  56.7 9.1 %collective-permute-done.4 = f32[1,4,128,128]{3,2,1,0:T(8,128)S(1)} collective-permute-done((f32[1,4,128,128]{3,2,1,0:T(8,128)S(1)}, f32[1,4,128,128]{3,2,1,0:T(8,128)S(1)}, u32[]{:S(2)}, u32[]{:S(2)}) %collective-permute-start.4) | collective-permute-done | bytes 262176 | tf_op jit(solution)/shard_map/ppermute | solution.py:46
  65.8 9.1 %collective-permute-done.5 = f32[1,4,128,128]{3,2,1,0:T(8,128)S(1)} collective-permute-done((f32[1,4,128,128]{3,2,1,0:T(8,128)S(1)}, f32[1,4,128,128]{3,2,1,0:T(8,128)S(1)}, u32[]{:S(2)}, u32[]{:S(2)}) %collective-permute-start.5) | collective-permute-done | bytes 262176 | tf_op jit(solution)/shard_map/ppermute | solution.py:46
  74.9 9.1 %collective-permute-done.6 = f32[1,4,128,128]{3,2,1,0:T(8,128)S(1)} collective-permute-done((f32[1,4,128,128]{3,2,1,0:T(8,128)S(1)}, f32[1,4,128,128]{3,2,1,0:T(8,128)S(1)}, u32[]{:S(2)}, u32[]{:S(2)}) %collective-permute-start.6) | collective-permute-done | bytes 262176 | tf_op jit(solution)/shard_map/ppermute | solution.py:46
  84.1 0.5 copy-done.10
  84.7 1.1 constant_dynamic-update-slice_fusion.7
  85.8 1.0 constant_dynamic-update-slice_fusion.6
  86.8 1.0 constant_dynamic-update-slice_fusion.5
  87.8 1.0 constant_dynamic-update-slice_fusion.4
  88.8 1.0 constant_dynamic-update-slice_fusion.3
  89.7 1.0 constant_dynamic-update-slice_fusion.2
  90.8 1.1 dynamic-slice_select_fusion.1
  92.0 0.1 fusion.33
  92.1 0.1 fusion.31
  92.1 0.1 broadcast_or_fusion.1
  92.2 0.1 reshape.129
  92.3 1.7 reshape.153
  94.1 1.9 copy.51
  96.0 2.8 gather_fusion
  98.8 26.4 %all-reduce.4.cloned.1.call-done = f32[8,2,128,128]{3,2,1,0:T(8,128)} async-done(((f32[8,2,128,128]{3,2,1,0:T(8,128)}), f32[8,2,128,128]{3,2,1,0:T(8,128)}) %all-reduce.4.cloned.1.call-update) | async-done | bytes 1048592 | tf_op jit(solution)/shard_map/psum | solution.py:11
  125.2 7.5 %convolution_bitcast_fusion.1 = f32[8,4,128,128]{3,2,1,0:T(8,128)} fusion(f32[8,4,2,128,128]{4,3,2,1,0:T(8,128)} %bitcast.129, f32[8,2,128,128]{3,2,1,0:T(8,128)} %all-reduce.4.cloned.1.call-done), kind=kOutput, calls=%fused_computation.5 | convolution fusion | flops 1610612736 | bytes 7340032 | tf_op jit(solution)/shard_map/pjkab,pkbc->pjac/dot_general | solution.py:57
  132.9 5.4 %all_gather.20 = f32[2,128,128]{2,1,0:T(8,128)S(1)} all-gather(f32[2,32,128]{2,1,0:T(8,128)S(1)} %copy-done.13), channel_id=1, replica_groups=mesh['row'=4,'col'=8] {'row'}, dimensions={1}, use_global_device_ids=true | all-gather | bytes 163840 | tf_op jit(solution)/shard_map/all_gather | solution.py:71
  138.3 1.4 fusion.17
  139.8 61.1 %reduce-scatter.4.cloned.1.call-done = f32[1,4,128,128]{3,2,1,0:T(8,128)} async-done(((f32[8,4,128,128]{3,2,1,0:T(8,128)}), f32[1,4,128,128]{3,2,1,0:T(8,128)}) %reduce-scatter.4.cloned.1.call-update) | async-done | bytes 262160 | tf_op jit(solution)/shard_map/reduce_scatter | solution.py:56
  200.9 1.0 neg.18
  201.9 1.2 fusion.8
  203.1 2.7 convolution_bitcast_fusion.4
  205.8 70.5 %all-gather.2.cloned.1.call-done = f32[16,4,128,128]{3,2,1,0:T(8,128)} async-done(((f32[2,4,128,128]{3,2,1,0:T(8,128)}), f32[16,4,128,128]{3,2,1,0:T(8,128)}) %all-gather.2.cloned.1.call-update) | async-done | bytes 4194320 | tf_op jit(solution)/shard_map/all_gather | solution.py:78
  276.3 3.2 dynamic-slice_select_fusion
  279.5 0.2 reduce-scatter.6.cloned.1.call-start
  279.7 0.1 copy.53
  279.8 0.1 broadcast_in_dim.39
  279.8 0.1 broadcast_in_dim_reshape.7
  279.9 0.1 copy.54
  280.0 0.1 broadcast_or_fusion
  280.1 0.1 reshape.135
  280.3 4.5 gather_fusion.1
  284.8 48.1 %all-reduce.6.cloned.1.call-done = (f32[1,128,128]{2,1,0:T(8,128)}, f32[16,2,128,128]{3,2,1,0:T(8,128)}, f32[2,128,128]{1,2,0:T(8,128)}) async-done(((f32[1,128,128]{2,1,0:T(8,128)}, f32[16,2,128,128]{3,2,1,0:T(8,128)}, f32[2,128,128]{1,2,0:T(8,128)}), (f32[1,128,128]{2,1,0:T(8,128)}, f32[16,2,128,128]{3,2,1,0:T(8,128)}, f32[2,128,128]{1,2,0:T(8,128)})) %all-reduce.6.cloned.1.call-update) | async-done | bytes 2293776 | tf_op jit(solution)/shard_map/psum | solution.py:67
  332.9 12.1 %convolution_bitcast_fusion = f32[16,4,128,128]{3,2,1,0:T(8,128)} fusion(f32[16,4,2,128,128]{4,3,2,1,0:T(8,128)} %bitcast.128, f32[16,2,128,128]{3,2,1,0:T(8,128)} %get-tuple-element.26), kind=kOutput, calls=%fused_computation.2 | convolution fusion | flops 3221225472 | bytes 14680064 | tf_op jit(solution)/shard_map/pjkab,pkbc->pjac/dot_general | solution.py:86
  345.1 0.0 reduce-scatter.8.cloned.1.call-start
  345.1 0.6 copy-done.16
  345.7 5.2 %all_gather.19 = f32[1,128,128]{2,1,0:T(8,128)S(1)} all-gather(f32[1,32,128]{2,1,0:T(8,128)S(1)} %copy-done.16), channel_id=1, replica_groups=mesh['row'=4,'col'=8] {'row'}, dimensions={1}, use_global_device_ids=true | all-gather | bytes 81920 | tf_op jit(solution)/shard_map/all_gather | solution.py:37
  351.0 5.4 %all_gather.22 = f32[2,128,128]{2,1,0:T(8,128)S(1)} all-gather(f32[2,32,128]{2,1,0:T(8,128)S(1)} %copy-done.14), channel_id=1, replica_groups=mesh['row'=4,'col'=8] {'row'}, dimensions={1}, use_global_device_ids=true | all-gather | bytes 163840 | tf_op jit(solution)/shard_map/all_gather | solution.py:70
  356.4 5.4 %all_gather.23 = f32[2,128,128]{2,1,0:T(8,128)S(1)} all-gather(f32[2,32,128]{2,1,0:T(8,128)S(1)} %copy-done.15), channel_id=1, replica_groups=mesh['row'=4,'col'=8] {'row'}, dimensions={1}, use_global_device_ids=true | all-gather | bytes 163840 | tf_op jit(solution)/shard_map/all_gather | solution.py:72
  361.8 0.4 fusion.19
  362.2 0.3 fusion.22
  362.5 0.4 fusion.38
  362.9 0.3 fusion.9
  363.2 70.2 %reduce-scatter.6.cloned.1.call-done = f32[2,4,128,128]{3,2,1,0:T(8,128)} async-done(((f32[16,4,128,128]{3,2,1,0:T(8,128)}), f32[2,4,128,128]{3,2,1,0:T(8,128)}) %reduce-scatter.6.cloned.1.call-update) | async-done | bytes 524304 | tf_op jit(solution)/shard_map/reduce_scatter | solution.py:85
  433.4 1.6 fusion.3
  435.0 1.7 fusion.4
  436.7 0.3 fusion.6
  437.0 0.1 constant_dynamic-slice_fusion
  437.1 0.7 copy.63
  437.8 0.6 constant_dynamic-slice_fusion.1
  438.4 17.8 %reduce-scatter.8.cloned.1.call-done = f32[2,32,128]{2,1,0:T(8,128)} async-done(((f32[2,128,128]{2,1,0:T(8,128)}), f32[2,32,128]{2,1,0:T(8,128)}) %reduce-scatter.8.cloned.1.call-update) | async-done | bytes 32784 | tf_op jit(solution)/shard_map/reduce_scatter | solution.py:114
  456.2 1.0 convolution_add_fusion
  457.2 0.9 convolution_subtract_fusion
  (63 shorter events, 0.6 us)
Async XLA Ops:
  7.2 131.1 %copy-start = (f32[2,4,128,128]{3,2,1,0:T(8,128)S(1)}, f32[2,4,128,128]{3,2,1,0:T(8,128)}, u32[]{:S(2)}) copy-start(f32[2,4,128,128]{3,2,1,0:T(8,128)} %param.14) | copy-start | bytes 1572868
  7.2 118.1 %all-reduce.4.cloned.1.call-start = ((), (), s32[]{:S(2)}) async-start(), calls=%async_computation.3 | async-start | bytes 2097152 | tf_op jit(solution)/shard_map/psum | solution.py:11
  15.1 11.8 %collective-permute-start = (f32[1,4,128,128]{3,2,1,0:T(8,128)S(1)}, f32[1,4,128,128]{3,2,1,0:T(8,128)S(1)}, u32[]{:S(2)}, u32[]{:S(2)}) collective-permute-start(f32[1,4,128,128]{3,2,1,0:T(8,128)S(1)} %bitcast.130), channel_id=1, source_target_pairs={{0,1},{1,2},{2,3},{3,4},{4,5},{5,6},{6,7},{7,0},{8,9},{9,10},{10,1... | collective-permute-start | bytes 786440 | tf_op jit(solution)/shard_map/ppermute | solution.py:46
  27.0 10.8 %collective-permute-start.1 = (f32[1,4,128,128]{3,2,1,0:T(8,128)S(1)}, f32[1,4,128,128]{3,2,1,0:T(8,128)S(1)}, u32[]{:S(2)}, u32[]{:S(2)}) collective-permute-start(f32[1,4,128,128]{3,2,1,0:T(8,128)S(1)} %collective-permute-done), channel_id=1, source_target_pairs={{0,1},{1,2},{2,3},{3,4},{4,5},{5,6},{6,7},{7,0},{8,9},{9,10},{10,1... | collective-permute-start | bytes 786440 | tf_op jit(solution)/shard_map/ppermute | solution.py:46
  37.7 46.3 %copy-start.5 = (f32[1,4,128,128]{3,2,1,0:T(8,128)}, f32[1,4,128,128]{3,2,1,0:T(8,128)S(1)}, u32[]{:S(2)}) copy-start(f32[1,4,128,128]{3,2,1,0:T(8,128)S(1)} %collective-permute-done.1) | copy-start | bytes 786436
  37.7 9.9 %collective-permute-start.2 = (f32[1,4,128,128]{3,2,1,0:T(8,128)S(1)}, f32[1,4,128,128]{3,2,1,0:T(8,128)S(1)}, u32[]{:S(2)}, u32[]{:S(2)}) collective-permute-start(f32[1,4,128,128]{3,2,1,0:T(8,128)S(1)} %collective-permute-done.1), channel_id=1, source_target_pairs={{0,1},{1,2},{2,3},{3,4},{4,5},{5,6},{6,7},{7,0},{8,9},{9,10},{10,1... | collective-permute-start | bytes 786440 | tf_op jit(solution)/shard_map/ppermute | solution.py:46
  47.6 36.5 %copy-start.6 = (f32[1,4,128,128]{3,2,1,0:T(8,128)}, f32[1,4,128,128]{3,2,1,0:T(8,128)S(1)}, u32[]{:S(2)}) copy-start(f32[1,4,128,128]{3,2,1,0:T(8,128)S(1)} %collective-permute-done.2) | copy-start | bytes 786436
  47.6 9.1 %collective-permute-start.3 = (f32[1,4,128,128]{3,2,1,0:T(8,128)S(1)}, f32[1,4,128,128]{3,2,1,0:T(8,128)S(1)}, u32[]{:S(2)}, u32[]{:S(2)}) collective-permute-start(f32[1,4,128,128]{3,2,1,0:T(8,128)S(1)} %collective-permute-done.2), channel_id=1, source_target_pairs={{0,1},{1,2},{2,3},{3,4},{4,5},{5,6},{6,7},{7,0},{8,9},{9,10},{10,1... | collective-permute-start | bytes 786440 | tf_op jit(solution)/shard_map/ppermute | solution.py:46
  56.7 27.4 %copy-start.7 = (f32[1,4,128,128]{3,2,1,0:T(8,128)}, f32[1,4,128,128]{3,2,1,0:T(8,128)S(1)}, u32[]{:S(2)}) copy-start(f32[1,4,128,128]{3,2,1,0:T(8,128)S(1)} %collective-permute-done.3) | copy-start | bytes 786436
  56.7 9.1 %collective-permute-start.4 = (f32[1,4,128,128]{3,2,1,0:T(8,128)S(1)}, f32[1,4,128,128]{3,2,1,0:T(8,128)S(1)}, u32[]{:S(2)}, u32[]{:S(2)}) collective-permute-start(f32[1,4,128,128]{3,2,1,0:T(8,128)S(1)} %collective-permute-done.3), channel_id=1, source_target_pairs={{0,1},{1,2},{2,3},{3,4},{4,5},{5,6},{6,7},{7,0},{8,9},{9,10},{10,1... | collective-permute-start | bytes 786440 | tf_op jit(solution)/shard_map/ppermute | solution.py:46
  65.8 18.3 %copy-start.8 = (f32[1,4,128,128]{3,2,1,0:T(8,128)}, f32[1,4,128,128]{3,2,1,0:T(8,128)S(1)}, u32[]{:S(2)}) copy-start(f32[1,4,128,128]{3,2,1,0:T(8,128)S(1)} %collective-permute-done.4) | copy-start | bytes 786436
  65.8 9.1 %collective-permute-start.5 = (f32[1,4,128,128]{3,2,1,0:T(8,128)S(1)}, f32[1,4,128,128]{3,2,1,0:T(8,128)S(1)}, u32[]{:S(2)}, u32[]{:S(2)}) collective-permute-start(f32[1,4,128,128]{3,2,1,0:T(8,128)S(1)} %collective-permute-done.4), channel_id=1, source_target_pairs={{0,1},{1,2},{2,3},{3,4},{4,5},{5,6},{6,7},{7,0},{8,9},{9,10},{10,1... | collective-permute-start | bytes 786440 | tf_op jit(solution)/shard_map/ppermute | solution.py:46
  74.9 9.2 %copy-start.9 = (f32[1,4,128,128]{3,2,1,0:T(8,128)}, f32[1,4,128,128]{3,2,1,0:T(8,128)S(1)}, u32[]{:S(2)}) copy-start(f32[1,4,128,128]{3,2,1,0:T(8,128)S(1)} %collective-permute-done.5) | copy-start | bytes 786436
  74.9 9.1 %collective-permute-start.6 = (f32[1,4,128,128]{3,2,1,0:T(8,128)S(1)}, f32[1,4,128,128]{3,2,1,0:T(8,128)S(1)}, u32[]{:S(2)}, u32[]{:S(2)}) collective-permute-start(f32[1,4,128,128]{3,2,1,0:T(8,128)S(1)} %collective-permute-done.5), channel_id=1, source_target_pairs={{0,1},{1,2},{2,3},{3,4},{4,5},{5,6},{6,7},{7,0},{8,9},{9,10},{10,1... | collective-permute-start | bytes 786440 | tf_op jit(solution)/shard_map/ppermute | solution.py:46
  83.9 0.7 copy-start.10
  84.7 7.3 %copy-start.17 = (s32[8,16]{1,0:T(8,128)S(1)}, s32[8,16]{1,0:T(8,128)}, u32[]{:S(2)}) copy-start(s32[8,16]{1,0:T(8,128)} %param.10) | copy-start | bytes 1540
  84.7 7.7 %copy-start.3 = (f32[1024,512]{1,0:T(8,128)S(1)}, f32[1024,512]{1,0:T(8,128)}, u32[]{:S(2)}) copy-start(f32[1024,512]{1,0:T(8,128)} %param.9) | copy-start | bytes 6291460
  91.9 109.0 %reduce-scatter.4.cloned.1.call-start = ((), (), s32[]{:S(2)}) async-start(), calls=%async_computation.4 | async-start | bytes 2359296 | tf_op jit(solution)/shard_map/reduce_scatter | solution.py:56
  125.2 7.6 %copy-start.13 = (f32[2,32,128]{2,1,0:T(8,128)S(1)}, f32[2,32,128]{2,1,0:T(8,128)}, u32[]{:S(2)}) copy-start(f32[2,32,128]{2,1,0:T(8,128)} %param.16) | copy-start | bytes 98308
  132.8 143.4 %all-gather.2.cloned.1.call-start = ((), (), s32[]{:S(2)}) async-start(), calls=%async_computation.5 | async-start | bytes 4718592 | tf_op jit(solution)/shard_map/all_gather | solution.py:78
  139.7 193.2 %all-reduce.6.cloned.1.call-start = ((), (), s32[]{:S(2)}) async-start(), calls=%async_computation.8 | async-start | bytes 4587520 | tf_op jit(solution)/shard_map/psum | solution.py:67
  201.9 231.5 %copy-start.2 = (f32[1,4,128,128]{3,2,1,0:T(8,128)}, f32[1,4,128,128]{3,2,1,0:T(8,128)S(1)}, u32[]{:S(2)}) copy-start(f32[1,4,128,128]{3,2,1,0:T(8,128)S(1)} %neg.18) | copy-start | bytes 786436
  279.5 153.9 %reduce-scatter.6.cloned.1.call-start = ((), (), s32[]{:S(2)}) async-start(), calls=%async_computation.6 | async-start | bytes 4718592 | tf_op jit(solution)/shard_map/reduce_scatter | solution.py:85
  345.0 0.7 copy-start.16
  345.0 5.9 %copy-start.14 = (f32[2,32,128]{2,1,0:T(8,128)S(1)}, f32[2,32,128]{2,1,0:T(8,128)}, u32[]{:S(2)}) copy-start(f32[2,32,128]{2,1,0:T(8,128)} %param.15) | copy-start | bytes 98308
  345.0 11.4 %copy-start.15 = (f32[2,32,128]{2,1,0:T(8,128)S(1)}, f32[2,32,128]{2,1,0:T(8,128)}, u32[]{:S(2)}) copy-start(f32[2,32,128]{2,1,0:T(8,128)} %param.17) | copy-start | bytes 98308
  345.0 17.9 %copy-start.12 = (f32[1,128,128]{2,1,0:T(8,128)S(1)}, f32[1,128,128]{2,1,0:T(8,128)}, u32[]{:S(2)}) copy-start(f32[1,128,128]{2,1,0:T(8,128)} %get-tuple-element.25) | copy-start | bytes 196612
  345.0 90.0 %copy-start.1 = (f32[2,4,128,128]{3,2,1,0:T(8,128)S(1)}, f32[2,4,128,128]{3,2,1,0:T(8,128)}, u32[]{:S(2)}) copy-start(f32[2,4,128,128]{3,2,1,0:T(8,128)} %fusion.17) | copy-start | bytes 1572868
  345.0 91.7 %copy-start.11 = (f32[2,128,128]{1,2,0:T(8,128)S(1)}, f32[2,128,128]{1,2,0:T(8,128)}, u32[]{:S(2)}) copy-start(f32[2,128,128]{1,2,0:T(8,128)} %get-tuple-element.27) | copy-start | bytes 393220
  345.1 111.2 %reduce-scatter.8.cloned.1.call-start = ((), (), s32[]{:S(2)}) async-start(), calls=%async_computation.7 | async-start | bytes 163840 | tf_op jit(solution)/shard_map/reduce_scatter | solution.py:114
  435.0 23.1 %copy-start.4 = (f32[2,4,128,128]{3,2,1,0:T(8,128)}, f32[2,4,128,128]{3,2,1,0:T(8,128)S(1)}, u32[]{:S(2)}) copy-start(f32[2,4,128,128]{3,2,1,0:T(8,128)S(1)} %fusion.3) | copy-start | bytes 1572868
Sparse Core Ops, SparseCore 0:
  92.0 33.1 all-reduce.3
  132.9 67.9 reduce-scatter.3
  203.8 72.3 all-gather.1
  279.6 53.2 all-reduce.5
  345.2 88.1 reduce-scatter.5
  436.8 19.3 reduce-scatter.7
